TPU v7x, 32 devices: a whole 2x2x4 slice. The times are simulated.
32 devices in a mesh: dp: 8 (over y, x, core), ctx: 4 (over z).
Axes of the slice: x: 2, y: 2, z: 4, core: 2. Of those that a mesh axis runs over, the one named last changes fastest.
Arguments:
- queries: bfloat16 [4096, 2048], P(('dp', 'ctx')), may hold values from -120 to 120
- keys: bfloat16 [4096, 512], P(('dp', 'ctx')), may hold values from -5.5 to 5.5
- values: bfloat16 [4096, 512], P(('dp', 'ctx')), may hold values from -6 to 6
- output_gradient: bfloat16 [4096, 2048], P(('dp', 'ctx')), may hold values from -6 to 6
- doc_blocks: int32 [16], P('dp'), may hold values from 1 to 3, 32 in all
- doc_pad: int32 [16], P('dp'), may hold values from 0 to 127
Outputs:
- attn_out: bfloat16 [4096, 2048], P(('dp', 'ctx'))
- grad_queries: bfloat16 [4096, 2048], P(('dp', 'ctx'))
- grad_keys: bfloat16 [4096, 512], P(('dp', 'ctx'))
- grad_values: bfloat16 [4096, 512], P(('dp', 'ctx'))
All inputs are finite; a program needn't handle non-finite values. No bound on the sum of `doc_blocks` on one device may be relied on, other than what follows from the above.
Results may differ from a plain program's by a relative error of at most 0.02.
Values may be sent and summed in bfloat16 or wider, within the bound.
No kernel may reach another device: no remote copies, remote signals or barrier semaphores. Data moves between devices by JAX's collectives and lax.ppermute only.
A program may use at most 64 MiB of HBM per device.

v0:
```python
import jax
import jax.numpy as jnp
from jax import lax
from jax.sharding import PartitionSpec as P

QUERY_HEADS = 16
KEY_VALUE_HEADS = 4
HEAD_SIZE = 128
MOST_DOC_BLOCKS = 3


def passed_along(array, axis, by):
    count = lax.axis_size(axis)
    pairs = [(i, i + by) for i in range(count) if 0 <= i + by < count]
    return lax.ppermute(array, axis, pairs)


def block_meta(block_ids, starts, doc_sizes, doc_pads, token_rows, block_count):
    in_range = (block_ids >= 0) & (block_ids < block_count)
    doc_index = jnp.sum((starts[None, :] <= block_ids[:, None]).astype(jnp.int32), axis=1) - 1
    doc_index = jnp.where(in_range, doc_index, -1)
    one_hot = jnp.arange(starts.shape[0], dtype=jnp.int32)[None, :] == doc_index[:, None]
    doc_ends = jnp.sum(
        jnp.where(one_hot, (starts + doc_sizes)[None, :] * token_rows - doc_pads[None, :], 0),
        axis=1,
    )
    positions = block_ids[:, None] * token_rows + jnp.arange(token_rows, dtype=jnp.int32)[None, :]
    is_valid = (positions < doc_ends[:, None]) & in_range[:, None]
    doc_ids = jnp.broadcast_to(doc_index[:, None], positions.shape)
    return (doc_ids.reshape(-1), positions.reshape(-1), is_valid.reshape(-1))


def allowed_pairs(query_info, key_info):
    same_doc = query_info[0][:, None] == key_info[0][None, :]
    causal = key_info[1][None, :] <= query_info[1][:, None]
    return same_doc & causal & query_info[2][:, None] & key_info[2][None, :]


def scores_of(query_rows, key_rows, score_scale):
    return (
        jnp.einsum("tkgd,skd->kgts", query_rows, key_rows, preferred_element_type=jnp.float32)
        * score_scale
    )


def softmax_parts(score_f32, pair_mask, query_valid):
    masked = jnp.where(pair_mask, score_f32, -jnp.inf)
    row_peak = jnp.where(query_valid, jnp.max(masked, axis=-1), 0.0)
    row_total = jnp.sum(
        jnp.where(pair_mask, jnp.exp(score_f32 - row_peak[..., None]), 0.0), axis=-1
    )
    log_total = row_peak + jnp.log(jnp.where(query_valid, row_total, 1.0))
    weight = jnp.where(pair_mask, jnp.exp(score_f32 - log_total[..., None]), 0.0)
    return (log_total, weight)


def fetch_back(payload, offset_step):
    return passed_along(payload, ("dp", "ctx"), offset_step)


def send_terms(payload, offset_step):
    return passed_along(payload, ("dp", "ctx"), offset_step)


def on_device(queries, keys, values, output_gradient, doc_blocks, doc_pad):
    token_rows = queries.shape[0]
    head_group_width = QUERY_HEADS // KEY_VALUE_HEADS
    score_scale = HEAD_SIZE ** (-0.5)
    backward_distance = MOST_DOC_BLOCKS - 1
    block_count = lax.axis_size("dp") * lax.axis_size("ctx")
    my_block = lax.axis_index("dp") * lax.axis_size("ctx") + lax.axis_index("ctx")
    doc_sizes, doc_pads = (
        lax.all_gather(doc_blocks, "dp", axis=0, tiled=True),
        lax.all_gather(doc_pad, "dp", axis=0, tiled=True),
    )
    starts = jnp.cumsum(doc_sizes) - doc_sizes

    def meta(block_ids):
        return block_meta(block_ids, starts, doc_sizes, doc_pads, token_rows, block_count)

    single = my_block + jnp.zeros((1,), jnp.int32)
    span = jnp.arange(MOST_DOC_BLOCKS, dtype=jnp.int32)
    own_info = meta(single)
    pair_mask = allowed_pairs(own_info, meta(my_block - backward_distance + span))
    key_value = jnp.stack([keys, values])
    pieces = []
    for offset_step in range(backward_distance, 0, -1):
        pieces.append(fetch_back(key_value, offset_step))
    pieces.append(key_value)
    neighbor_key_values = jnp.concatenate(pieces, axis=1)
    neighbor_keys = neighbor_key_values[0].reshape(
        MOST_DOC_BLOCKS * token_rows, KEY_VALUE_HEADS, HEAD_SIZE
    )
    neighbor_values = neighbor_key_values[1].reshape(
        MOST_DOC_BLOCKS * token_rows, KEY_VALUE_HEADS, HEAD_SIZE
    )
    query_head_rows = queries.reshape(token_rows, KEY_VALUE_HEADS, head_group_width, HEAD_SIZE)
    gradient_heads = output_gradient.reshape(
        token_rows, KEY_VALUE_HEADS, head_group_width, HEAD_SIZE
    )
    score_f32 = scores_of(query_head_rows, neighbor_keys, score_scale)
    log_total, weight = softmax_parts(score_f32, pair_mask, own_info[2])
    weight_bf16 = weight.astype(jnp.bfloat16)
    attn = jnp.einsum(
        "kgts,skd->tkgd", weight_bf16, neighbor_values, preferred_element_type=jnp.float32
    ).astype(jnp.bfloat16)
    delta_rows = jnp.einsum(
        "tkgd,tkgd->kgt", gradient_heads, attn, preferred_element_type=jnp.float32
    )
    dprob = jnp.einsum(
        "tkgd,skd->kgts", gradient_heads, neighbor_values, preferred_element_type=jnp.float32
    )
    dscore = (weight * (dprob - delta_rows[..., None])).astype(jnp.bfloat16)
    grad_q = (
        jnp.einsum("kgts,skd->tkgd", dscore, neighbor_keys, preferred_element_type=jnp.float32)
        * score_scale
    )
    summand_keys = jnp.einsum(
        "kgts,tkgd->skd", dscore, query_head_rows, preferred_element_type=jnp.float32
    )
    summand_values = jnp.einsum(
        "kgts,tkgd->skd", weight_bf16, gradient_heads, preferred_element_type=jnp.float32
    )
    terms = jnp.stack([summand_keys, summand_values]).reshape(
        2, MOST_DOC_BLOCKS, token_rows, KEY_VALUE_HEADS * HEAD_SIZE
    )
    gathered = terms[:, backward_distance]
    for offset_step in range(1, backward_distance + 1):
        gathered = gathered + send_terms(terms[:, backward_distance - offset_step], -offset_step)
    grad_k = (gathered[0] * score_scale).astype(jnp.bfloat16)
    grad_v = gathered[1].astype(jnp.bfloat16)
    return (
        attn.reshape(token_rows, QUERY_HEADS * HEAD_SIZE),
        grad_q.astype(jnp.bfloat16).reshape(token_rows, QUERY_HEADS * HEAD_SIZE),
        grad_k,
        grad_v,
    )


def solution(mesh):
    in_specs = (
        P(("dp", "ctx"), None),
        P(("dp", "ctx"), None),
        P(("dp", "ctx"), None),
        P(("dp", "ctx"), None),
        P("dp"),
        P("dp"),
    )
    out_specs = (
        P(("dp", "ctx"), None),
        P(("dp", "ctx"), None),
        P(("dp", "ctx"), None),
        P(("dp", "ctx"), None),
    )
    return jax.shard_map(
        on_device, mesh=mesh, in_specs=in_specs, out_specs=out_specs, check_vma=False
    )
```

profile of v0, /device:TPU:27, one launch (start us, length us, event | category | flops | bytes accessed | tf_op | source)
XLA Modules:
  0.0 94.3 jit_solution(15968947168281493260)
XLA Ops:
  0.6 1.0 %copy.40 = bf16[128,512]{0,1:T(8,128)(2,1)S(1)} copy(bf16[128,512]{1,0:T(8,128)(2,1)} %param.8) | data formatting | bytes 262144 | tf_op args[2]
  1.7 1.0 %copy.39 = bf16[128,512]{0,1:T(8,128)(2,1)S(1)} copy(bf16[128,512]{1,0:T(8,128)(2,1)} %param.7) | data formatting | bytes 262144 | tf_op args[1]
  2.7 3.3 %collective-permute-start.1 = (bf16[2,128,512]{1,2,0:T(8,128)(2,1)S(1)}, bf16[2,128,512]{1,2,0:T(8,128)(2,1)S(1)}, u32[]{:S(2)}, u32[]{:S(2)}) collective-permute-start(bf16[2,128,512]{1,2,0:T(8,128)(2,1)S(1)} %pad_maximum_fusion), channel_id=1, source_target_pairs={{0,1},{1,2},{2,3},{3,4},{4,5},{5,6},{6,7},{7,8},{8,9},{9,10},{10,1... | collective-permute-start | bytes 786440 | tf_op jit(solution)/shard_map/ppermute | solution.py:15
  6.1 3.6 %collective-permute-start = (bf16[2,128,512]{1,2,0:T(8,128)(2,1)S(1)}, bf16[2,128,512]{1,2,0:T(8,128)(2,1)S(1)}, u32[]{:S(2)}, u32[]{:S(2)}) collective-permute-start(bf16[2,128,512]{1,2,0:T(8,128)(2,1)S(1)} %pad_maximum_fusion), channel_id=1, source_target_pairs={{0,2},{1,3},{2,4},{3,5},{4,6},{5,7},{6,8},{7,9},{8,10},{9,11},{10,... | collective-permute-start | bytes 786440 | tf_op jit(solution)/shard_map/ppermute | solution.py:15
  9.7 0.1 add_bitcast_fusion
  9.8 1.2 %dynamic-slice = u32[1]{0:T(128)} dynamic-slice(u32[32]{0:T(128)} %constant.54, u32[]{:T(128)S(6)} %add.100), dynamic_slice_sizes={1} | dynamic-slice | bytes 12
  11.7 0.9 dynamic-update-slice.1
  12.6 0.8 dynamic-update-slice
  13.4 5.3 %all-reduce.2 = (s32[16]{0:T(128)S(1)}, s32[16]{0:T(128)S(1)}) all-reduce(s32[16]{0:T(128)S(1)} %dynamic-update-slice.1, s32[16]{0:T(128)S(1)} %dynamic-update-slice), channel_id=1, replica_groups=mesh['dp'=8,'ctx'=4] {'dp'}, use_global_device_ids=true, to_apply=%add.1 | all-reduce | flops 32 | bytes 256
  18.7 0.1 copy.41
  18.8 0.1 reduce.5
  19.0 0.6 fusion.23
  20.2 0.6 fusion.24
  20.9 0.2 convert_reduce_fusion
  21.1 0.1 broadcast_bitcast_fusion
  21.2 0.2 select_reduce_fusion
  21.3 0.1 fusion.22
  21.4 0.7 compare_and_fusion
  22.1 2.2 %reshape.181 = bf16[128,4,4,128]{3,2,1,0:T(4,128)(2,1)} reshape(bf16[128,2048]{1,0:T(8,128)(2,1)} %param.6) | data formatting | bytes 1048576 | tf_op jit(solution)/shard_map/reshape | solution.py:97
  24.3 2.2 %reshape.183 = bf16[128,4,4,128]{3,2,1,0:T(4,128)(2,1)} reshape(bf16[128,2048]{1,0:T(8,128)(2,1)} %param.9) | data formatting | bytes 1048576 | tf_op jit(solution)/shard_map/reshape | solution.py:98
  26.5 0.0 copy-start.2
  26.5 0.2 and_and_fusion
  26.7 0.0 copy-start.7
  26.7 0.0 collective-permute-done.1
  26.7 0.0 collective-permute-done
  26.7 0.1 maximum_maximum_fusion
  26.8 0.1 fusion.29
  26.9 0.0 copy-start.6
  26.9 0.6 copy-done.2
  27.5 0.7 fusion.2
  28.2 0.7 fusion.5
  28.9 0.0 copy-done.7
  28.9 0.0 copy-done.6
  28.9 1.9 %bitcast_convert_fusion = (f32[4,4,128,128]{2,3,1,0:T(8,128)}, bf16[4,128,4,128]{3,1,2,0:T(8,128)(2,1)}) fusion(bf16[384,4,128,1]{0,2,3,1:T(8,128)(2,1)S(1)} %bitcast.111, f32[4,384,128,4]{2,1,3,0:T(8,128)S(1)} %get-tuple-element.29, f32[4,4,128]{2,1,0:T(4,128)S(1)} %log_add_fusion, pred[128,384]{0,1:T(8,128)(4,1)S(1)} %and_and_fusion), kind=kOutput, calls=%fused_computation.25 | convolution fusion | flops 204996608 | bytes 5169152 | tf_op jit(solution)/shard_map/kgts,skd->tkgd/dot_general | solution.py:104
  30.9 2.7 %copy.65 = f32[4,4,128,128]{3,1,0,2:T(4,128)} copy(f32[4,4,128,128]{2,3,1,0:T(8,128)} %get-tuple-element.30) | data formatting | bytes 2097152
  33.5 2.8 %convolution_bitcast_fusion = f32[384,4,128]{2,0,1:T(8,128)} fusion(bf16[128,4,4,128]{3,2,1,0:T(4,128)(2,1)} %reshape.183, f32[4,384,128,4]{2,1,3,0:T(8,128)S(1)} %get-tuple-element.29, f32[4,4,128]{2,1,0:T(4,128)S(1)} %log_add_fusion, pred[128,384]{0,1:T(8,128)(4,1)} %copy-done.7), kind=kOutput, calls=%fused_computation.15 | convolution fusion | flops 204472320 | bytes 4513792 | tf_op jit(solution)/shard_map/kgts,tkgd->skd/dot_general | solution.py:121
  36.4 0.0 copy-done.4
  36.4 0.0 copy-done.5
  36.4 1.6 %multiply_reduce_fusion = f32[4,4,128]{1,0,2:T(4,128)} fusion(f32[4,4,128,128]{3,1,0,2:T(4,128)S(1)} %copy-done.4, bf16[128,4,4,128]{3,2,1,0:T(4,128)(2,1)S(1)} %copy-done.5), kind=kLoop, calls=%fused_computation.18 | loop fusion | flops 784384 | bytes 1581056
  37.9 1.0 %copy.66 = f32[4,4,128]{2,1,0:T(4,128)S(1)} copy(f32[4,4,128]{1,0,2:T(4,128)} %multiply_reduce_fusion) | data formatting | bytes 16384 | tf_op jit(solution)/shard_map/tkgd,tkgd->kgt/dot_general | solution.py:107
  39.0 2.4 %fusion.1 = bf16[4,4,128,384]{2,3,1,0:T(8,128)(2,1)S(1)} fusion(f32[4,384,128,4]{2,1,3,0:T(8,128)S(1)} %get-tuple-element.29, bf16[384,4,128,1]{0,2,3,1:T(8,128)(2,1)} %bitcast.112, f32[4,4,128]{2,1,0:T(4,128)S(1)} %copy.66, f32[4,4,128]{2,1,0:T(4,128)S(1)} %log_add_fusion, pred[128,384]{0,1:T(8,128)(4,1)} %copy-done.7, bf16[128,4,4,128]{3,2,1,0:T(4,128)(2,1)} %reshape.183), kind=kOutput, calls=%fused_computation.2 | convolution fusion | flops 206045184 | bytes 5701632 | tf_op jit(solution)/shard_map/tkgd,skd->kgts/dot_general | solution.py:110
  41.4 0.0 copy-start
  41.4 1.1 %copy-done = bf16[4,4,128,384]{2,3,1,0:T(8,128)(2,1)} copy-done((bf16[4,4,128,384]{2,3,1,0:T(8,128)(2,1)}, bf16[4,4,128,384]{2,3,1,0:T(8,128)(2,1)S(1)}, u32[]{:S(2)}) %copy-start) | copy-done | bytes 1572888
  42.5 0.0 copy-done.3
  42.5 0.6 convolution_bitcast_fusion.1
  43.1 0.5 copy.49
  43.6 0.3 stack.21
  44.0 0.1 constant_dynamic-update-slice_fusion.1
  44.0 0.0 copy-done.8
  44.0 1.4 %copy.51 = f32[384,4,128]{2,1,0:T(4,128)} copy(f32[384,4,128]{2,0,1:T(8,128)S(1)} %copy-done.8) | data formatting | bytes 1572864 | tf_op jit(solution)/shard_map/kgts,tkgd->skd/transpose | solution.py:121
  45.4 2.5 %stack.22 = f32[1,3,128,512]{3,2,1,0:T(8,128)} reshape(f32[384,4,128]{2,1,0:T(4,128)} %copy.51) | data formatting | bytes 1572864 | tf_op jit(solution)/shard_map/stack | solution.py:124
  47.9 1.2 %constant_dynamic-update-slice_fusion = f32[2,3,128,512]{3,2,1,0:T(8,128)S(1)} fusion(f32[2,3,128,512]{3,2,1,0:T(8,128)S(1)} %constant_dynamic-update-slice_fusion.1, f32[1,3,128,512]{3,2,1,0:T(8,128)} %stack.22), kind=kLoop, calls=%fused_computation.39 | loop fusion | bytes 1572864 | tf_op jit(solution)/shard_map/stack | solution.py:124
  49.1 1.0 %slice_bitcast_fusion.1 = (f32[2,128,512]{2,1,0:T(8,128)}, f32[2,128,512]{2,1,0:T(8,128)}) fusion(f32[2,3,128,512]{3,2,1,0:T(8,128)S(1)} %constant_dynamic-update-slice_fusion), kind=kLoop, calls=%fused_computation.21 | loop fusion | bytes 2097152 | tf_op jit(solution)/shard_map/squeeze | solution.py:129
  50.1 3.2 %collective-permute-start.3 = (f32[2,128,512]{2,1,0:T(8,128)}, f32[2,128,512]{2,1,0:T(8,128)}, u32[]{:S(2)}, u32[]{:S(2)}) collective-permute-start(f32[2,128,512]{2,1,0:T(8,128)} %get-tuple-element.25), channel_id=1, source_target_pairs={{2,0},{3,1},{4,2},{5,3},{6,4},{7,5},{8,6},{9,7},{10,8},{11,9},{12,... | collective-permute-start | bytes 1572872 | tf_op jit(solution)/shard_map/ppermute | solution.py:15
  53.3 2.7 %collective-permute-start.2 = (f32[2,128,512]{2,1,0:T(8,128)}, f32[2,128,512]{2,1,0:T(8,128)}, u32[]{:S(2)}, u32[]{:S(2)}) collective-permute-start(f32[2,128,512]{2,1,0:T(8,128)} %get-tuple-element.24), channel_id=1, source_target_pairs={{1,0},{2,1},{3,2},{4,3},{5,4},{6,5},{7,6},{8,7},{9,8},{10,9},{11,1... | collective-permute-start | bytes 1572872 | tf_op jit(solution)/shard_map/ppermute | solution.py:15
  56.0 2.0 %copy.54 = bf16[128,2048]{1,0:T(8,128)(2,1)} copy(bf16[128,2048]{0,1:T(8,128)(2,1)} %bitcast.109) | data formatting | bytes 1048576
  58.0 0.0 copy-done.1
  58.0 1.2 %fusion.9 = bf16[4,128,4,128]{3,1,2,0:T(8,128)(2,1)} fusion(bf16[384,4,128,1]{0,2,3,1:T(8,128)(2,1)S(1)} %bitcast.108, bf16[4,4,128,384]{2,3,1,0:T(8,128)(2,1)S(1)} %copy-done.1), kind=kOutput, calls=%fused_computation.14 | convolution fusion | flops 201850880 | bytes 2490368 | tf_op jit(solution)/shard_map/kgts,skd->tkgd/dot_general | solution.py:115
  59.3 2.0 %copy.55 = bf16[128,2048]{1,0:T(8,128)(2,1)} copy(bf16[128,2048]{0,1:T(8,128)(2,1)} %bitcast.110) | data formatting | bytes 1048576
  61.3 30.3 %collective-permute-done.3 = f32[2,128,512]{2,1,0:T(8,128)} collective-permute-done((f32[2,128,512]{2,1,0:T(8,128)}, f32[2,128,512]{2,1,0:T(8,128)}, u32[]{:S(2)}, u32[]{:S(2)}) %collective-permute-start.3) | collective-permute-done | bytes 524320 | tf_op jit(solution)/shard_map/ppermute | solution.py:15
  91.6 0.0 collective-permute-done.2
  91.6 1.3 %fusion.11 = f32[2,128,512]{2,1,0:T(8,128)S(1)} fusion(f32[2,128,512]{2,1,0:T(8,128)} %collective-permute-done.3, f32[2,128,512]{2,1,0:T(8,128)} %collective-permute-done.2, f32[2,3,128,512]{3,2,1,0:T(8,128)S(1)} %constant_dynamic-update-slice_fusion), kind=kLoop, calls=%fused_computation.24 | loop fusion | flops 262144 | bytes 2097152 | tf_op jit(solution)/shard_map/add | solution.py:129
  92.9 0.7 fusion.18
  93.6 0.7 fusion.19
  (15 shorter events, 0.1 us)
Async XLA Ops:
  2.7 24.0 %collective-permute-start.1 = (bf16[2,128,512]{1,2,0:T(8,128)(2,1)S(1)}, bf16[2,128,512]{1,2,0:T(8,128)(2,1)S(1)}, u32[]{:S(2)}, u32[]{:S(2)}) collective-permute-start(bf16[2,128,512]{1,2,0:T(8,128)(2,1)S(1)} %pad_maximum_fusion), channel_id=1, source_target_pairs={{0,1},{1,2},{2,3},{3,4},{4,5},{5,6},{6,7},{7,8},{8,9},{9,10},{10,1... | collective-permute-start | bytes 786440 | tf_op jit(solution)/shard_map/ppermute | solution.py:15
  6.1 20.6 %collective-permute-start = (bf16[2,128,512]{1,2,0:T(8,128)(2,1)S(1)}, bf16[2,128,512]{1,2,0:T(8,128)(2,1)S(1)}, u32[]{:S(2)}, u32[]{:S(2)}) collective-permute-start(bf16[2,128,512]{1,2,0:T(8,128)(2,1)S(1)} %pad_maximum_fusion), channel_id=1, source_target_pairs={{0,2},{1,3},{2,4},{3,5},{4,6},{5,7},{6,8},{7,9},{8,10},{9,11},{10,... | collective-permute-start | bytes 786440 | tf_op jit(solution)/shard_map/ppermute | solution.py:15
  26.5 1.0 %copy-start.2 = (bf16[128,4,4,128]{3,2,1,0:T(4,128)(2,1)S(1)}, bf16[128,4,4,128]{3,2,1,0:T(4,128)(2,1)}, u32[]{:S(2)}) copy-start(bf16[128,4,4,128]{3,2,1,0:T(4,128)(2,1)} %reshape.181) | copy-start | bytes 1572868
  26.7 2.2 %copy-start.7 = (pred[128,384]{0,1:T(8,128)(4,1)}, pred[128,384]{0,1:T(8,128)(4,1)S(1)}, u32[]{:S(2)}) copy-start(pred[128,384]{0,1:T(8,128)(4,1)S(1)} %and_and_fusion) | copy-start | bytes 147460
  26.9 2.0 %copy-start.6 = (bf16[1,384,512]{1,2,0:T(8,128)(2,1)}, bf16[1,384,512]{1,2,0:T(8,128)(2,1)S(1)}, u32[]{:S(2)}) copy-start(bf16[1,384,512]{1,2,0:T(8,128)(2,1)S(1)} %get-tuple-element.27) | copy-start | bytes 1179652
  33.5 2.8 %copy-start.4 = (f32[4,4,128,128]{3,1,0,2:T(4,128)S(1)}, f32[4,4,128,128]{3,1,0,2:T(4,128)}, u32[]{:S(2)}) copy-start(f32[4,4,128,128]{3,1,0,2:T(4,128)} %copy.65) | copy-start | bytes 3145732
  33.5 2.8 %copy-start.5 = (bf16[128,4,4,128]{3,2,1,0:T(4,128)(2,1)S(1)}, bf16[128,4,4,128]{3,2,1,0:T(4,128)(2,1)}, u32[]{:S(2)}) copy-start(bf16[128,4,4,128]{3,2,1,0:T(4,128)(2,1)} %reshape.183) | copy-start | bytes 1572868
  39.0 3.6 %copy-start.3 = (bf16[128,4,4,128]{3,2,1,0:T(4,128)(2,1)S(1)}, bf16[128,4,4,128]{3,2,1,0:T(4,128)(2,1)}, u32[]{:S(2)}) copy-start(bf16[128,4,4,128]{3,2,1,0:T(4,128)(2,1)} %reshape.181) | copy-start | bytes 1572868
  41.4 1.2 %copy-start = (bf16[4,4,128,384]{2,3,1,0:T(8,128)(2,1)}, bf16[4,4,128,384]{2,3,1,0:T(8,128)(2,1)S(1)}, u32[]{:S(2)}) copy-start(bf16[4,4,128,384]{2,3,1,0:T(8,128)(2,1)S(1)} %fusion.1) | copy-start | bytes 4718596
  42.5 1.5 %copy-start.8 = (f32[384,4,128]{2,0,1:T(8,128)S(1)}, f32[384,4,128]{2,0,1:T(8,128)}, u32[]{:S(2)}) copy-start(f32[384,4,128]{2,0,1:T(8,128)} %convolution_bitcast_fusion) | copy-start | bytes 2359300
  45.4 12.6 %copy-start.1 = (bf16[4,4,128,384]{2,3,1,0:T(8,128)(2,1)S(1)}, bf16[4,4,128,384]{2,3,1,0:T(8,128)(2,1)}, u32[]{:S(2)}) copy-start(bf16[4,4,128,384]{2,3,1,0:T(8,128)(2,1)} %copy-done) | copy-start | bytes 4718596
  50.1 41.5 %collective-permute-start.3 = (f32[2,128,512]{2,1,0:T(8,128)}, f32[2,128,512]{2,1,0:T(8,128)}, u32[]{:S(2)}, u32[]{:S(2)}) collective-permute-start(f32[2,128,512]{2,1,0:T(8,128)} %get-tuple-element.25), channel_id=1, source_target_pairs={{2,0},{3,1},{4,2},{5,3},{6,4},{7,5},{8,6},{9,7},{10,8},{11,9},{12,... | collective-permute-start | bytes 1572872 | tf_op jit(solution)/shard_map/ppermute | solution.py:15
  53.3 38.3 %collective-permute-start.2 = (f32[2,128,512]{2,1,0:T(8,128)}, f32[2,128,512]{2,1,0:T(8,128)}, u32[]{:S(2)}, u32[]{:S(2)}) collective-permute-start(f32[2,128,512]{2,1,0:T(8,128)} %get-tuple-element.24), channel_id=1, source_target_pairs={{1,0},{2,1},{3,2},{4,3},{5,4},{6,5},{7,6},{8,7},{9,8},{10,9},{11,1... | collective-permute-start | bytes 1572872 | tf_op jit(solution)/shard_map/ppermute | solution.py:15
where the time goes:
time: 95 us; the launch traced here: 94.3 us
  waiting for transfers between devices  30.3 us (32%)
  local copies, waits for them, and re-layouts  26.8 us (28%)
  starting transfers between devices  12.8 us (13%)
  matrix products  9.68 us (10%)
  other arithmetic  7.23 us (8%)
  blocking collectives  5.32 us (6%)
  between operations  2.2 us (2%)
    ppermute x4, waiting for transfers between devices, passed_along(): return lax.ppermute(array, axis, pairs)  30.3 us
    unnamed x29, local copies, waits for them, and re-layouts  13.5 us
    ppermute x4, starting transfers between devices, passed_along(): return lax.ppermute(array, axis, pairs)  12.8 us
    unnamed x1, blocking collectives  5.32 us
    another operation x3, local copies, waits for them, and re-layouts, on_device(): jnp.stack([summand_keys, summand_values])  3.96 us
    dot_general x1, matrix products, on_device(): jnp.einsum('kgts,tkgd->skd', weight_bf16, gradient_heads, preferred_eleme...  2.82 us
    dot_general x1, matrix products, on_device(): jnp.einsum('tkgd,skd->kgts', gradient_heads, neighbor_values, preferred_e...  2.4 us
    reshape x1, local copies, waits for them, and re-layouts, on_device(): queries.reshape(token_rows, KEY_VALUE_HEADS, head_group_width, HEAD_SIZE)  2.2 us
  transfers between devices with their start and end apart: 4, of which 1 were waited for; matrix products, arithmetic and copies ran while one was open for 17% of the time, Pallas kernels for 0%

commit v1 on v0

v1 whole, which is shorter than its diff:
```python
import functools
import jax
import jax.numpy as jnp
from jax import lax
from jax.experimental import pallas as pl
from jax.experimental.pallas import tpu as pltpu
from jax.sharding import PartitionSpec as P

QUERY_HEADS = 16
KEY_VALUE_HEADS = 4
HEAD_SIZE = 128
MOST_DOC_BLOCKS = 3
GROUP = QUERY_HEADS // KEY_VALUE_HEADS
AXES = ("dp", "ctx")
LOG2E = 1.4426950408889634
NEG = -1e30
CHUNKS = 2
LANE_HEADS = 2


def rotated(array, by):
    count = lax.axis_size(AXES)
    return lax.ppermute(array, AXES, [(i, (i + by) % count) for i in range(count)])


def doc_bounds(codes_ref, block, rows):
    def step(i, carry):
        start, first, end = carry
        code = codes_ref[i]
        size = code // rows
        mine = (start <= block) & (block < start + size)
        first = jnp.where(mine, start, first)
        end = jnp.where(mine, (start + size) * rows - code % rows, end)
        return start + size, first, end

    zero = jnp.int32(0)
    _, first, end = lax.fori_loop(0, codes_ref.shape[0], step, (zero, zero, zero))
    return first, end


def dot(a, b, contract):
    return lax.dot_general(
        a, b, ((contract[:1], contract[1:]), ((), ())), preferred_element_type=jnp.float32
    )


def attend(heads, codes_ref, q_ref, do_ref, k0_ref, v0_ref, r1_ref, r2_ref, *rest):
    attn_ref, dq_ref, own_ref, t1_ref, t2_ref = rest[-5:]
    rows = q_ref.shape[0]
    size = HEAD_SIZE
    block = lax.axis_index("dp") * lax.axis_size("ctx") + lax.axis_index("ctx")
    first, end = doc_bounds(codes_ref, block, rows)
    scale = HEAD_SIZE ** (-0.5)
    bias1 = jnp.where(first <= block - 1, 0.0, NEG).astype(jnp.float32)
    bias2 = jnp.where(first <= block - 2, 0.0, NEG).astype(jnp.float32)
    width = LANE_HEADS * rows
    key_at = lax.broadcasted_iota(jnp.int32, (rows, width), 0)
    query_at = lax.broadcasted_iota(jnp.int32, (rows, width), 1) % rows
    causal = jnp.where(key_at <= query_at, 0.0, NEG).astype(jnp.float32)
    lane = lax.broadcasted_iota(jnp.int32, (1, width), 1) % rows
    valid = block * rows + lane < end
    for head in range(heads):
        cols = slice(head * size, (head + 1) * size)
        key = jnp.concatenate(
            [r2_ref[:rows, cols], r1_ref[:rows, cols], k0_ref[:, cols]], axis=0
        )
        value = jnp.concatenate(
            [r2_ref[rows:, cols], r1_ref[rows:, cols], v0_ref[:, cols]], axis=0
        )
        dk = dv = None
        for part in range(GROUP // LANE_HEADS):
            names = [head * GROUP + part * LANE_HEADS + i for i in range(LANE_HEADS)]
            q = jnp.concatenate([q_ref[:, n * size : (n + 1) * size] for n in names], axis=0)
            do = jnp.concatenate([do_ref[:, n * size : (n + 1) * size] for n in names], axis=0)
            score = dot(key, q, (1, 1)) * (scale * LOG2E)
            s2 = score[:rows] + bias2
            s1 = score[rows : 2 * rows] + bias1
            s0 = score[2 * rows :] + causal
            peak = jnp.max(jnp.maximum(jnp.maximum(s2, s1), s0), axis=0, keepdims=True)
            e2, e1, e0 = jnp.exp2(s2 - peak), jnp.exp2(s1 - peak), jnp.exp2(s0 - peak)
            total = jnp.sum(e2 + e1 + e0, axis=0, keepdims=True)
            inverse = jnp.where(valid, 1.0 / total, 0.0)
            weight = jnp.concatenate([e2, e1, e0], axis=0) * inverse
            dprob = dot(value, do, (1, 1))
            delta = jnp.sum(weight * dprob, axis=0, keepdims=True)
            dscore = (weight * (dprob - delta)).astype(jnp.bfloat16)
            weight = weight.astype(jnp.bfloat16)
            out = dot(value, weight, (0, 0))
            dq = dot(key, dscore, (0, 0)) * scale
            for i, n in enumerate(names):
                at = slice(n * size, (n + 1) * size)
                lanes = slice(i * rows, (i + 1) * rows)
                attn_ref[:, at] = out[:, lanes].T.astype(jnp.bfloat16)
                dq_ref[:, at] = dq[:, lanes].T.astype(jnp.bfloat16)
            dv_part = dot(weight, do, (1, 0))
            dk_part = dot(dscore, q, (1, 0))
            dv = dv_part if dv is None else dv + dv_part
            dk = dk_part if dk is None else dk + dk_part
        dk = dk * scale
        t2_ref[:rows, cols] = dk[:rows].astype(jnp.bfloat16)
        t2_ref[rows:, cols] = dv[:rows].astype(jnp.bfloat16)
        t1_ref[:rows, cols] = dk[rows : 2 * rows].astype(jnp.bfloat16)
        t1_ref[rows:, cols] = dv[rows : 2 * rows].astype(jnp.bfloat16)
        own_ref[:rows, cols] = dk[2 * rows :]
        own_ref[rows:, cols] = dv[2 * rows :]


def call_attend(chunk, codes, q, do, keys, values, r1, r2, before):
    rows, q_width = q.shape
    heads = KEY_VALUE_HEADS // CHUNKS
    wide = heads * GROUP * HEAD_SIZE
    narrow = heads * HEAD_SIZE
    vmem = pltpu.VMEM
    q_spec = pl.BlockSpec((rows, wide), lambda i: (0, chunk), memory_space=vmem)
    kv_spec = pl.BlockSpec((rows, narrow), lambda i: (0, chunk), memory_space=vmem)
    whole = pl.BlockSpec((2 * rows, narrow), lambda i: (0, 0), memory_space=vmem)
    any_spec = pl.BlockSpec(memory_space=pl.ANY)
    bf16 = jnp.bfloat16
    shape = jax.ShapeDtypeStruct
    return pl.pallas_call(
        functools.partial(attend, heads),
        grid=(1,),
        name=f"attend{chunk}",
        in_specs=[pl.BlockSpec(memory_space=pltpu.SMEM), q_spec, q_spec, kv_spec, kv_spec]
        + [whole, whole]
        + [any_spec] * len(before),
        out_specs=[q_spec, q_spec, whole, whole, whole],
        out_shape=[
            shape((rows, q_width), bf16),
            shape((rows, q_width), bf16),
            shape((2 * rows, narrow), jnp.float32),
            shape((2 * rows, narrow), bf16),
            shape((2 * rows, narrow), bf16),
        ],
        input_output_aliases={7 + i: i for i in range(len(before))},
        cost_estimate=pl.CostEstimate(
            flops=12 * rows * 3 * rows * wide, bytes_accessed=8 * rows * wide, transcendentals=0
        ),
    )(codes, q, do, keys, values, r1, r2, *before)


def finish(chunks, *refs):
    dk_ref, dv_ref = refs[-2:]
    rows = dk_ref.shape[0]
    for c in range(chunks):
        own, r1, r2 = refs[3 * c : 3 * c + 3]
        width = own.shape[1]
        total = own[...] + r1[...].astype(jnp.float32) + r2[...].astype(jnp.float32)
        dk_ref[:, c * width : (c + 1) * width] = total[:rows].astype(jnp.bfloat16)
        dv_ref[:, c * width : (c + 1) * width] = total[rows:].astype(jnp.bfloat16)


def on_device(queries, keys, values, output_gradient, doc_blocks, doc_pad):
    rows = queries.shape[0]
    width = KEY_VALUE_HEADS * HEAD_SIZE // CHUNKS
    per = doc_blocks.shape[0]
    parts = lax.axis_size("dp")
    code = doc_blocks * rows + doc_pad
    spread = jnp.tile(code, parts)
    owner = jnp.arange(per * parts, dtype=jnp.int32) // per
    codes = lax.psum(jnp.where(owner == lax.axis_index("dp"), spread, 0), "dp")
    payloads = [
        jnp.concatenate(
            [keys[:, c * width : (c + 1) * width], values[:, c * width : (c + 1) * width]], axis=0
        )
        for c in range(CHUNKS)
    ]
    arrived = [(rotated(p, 1), rotated(p, 2)) for p in payloads]
    before = ()
    gathered = []
    for c in range(CHUNKS):
        r1, r2 = arrived[c]
        attn, dq, own, t1, t2 = call_attend(
            c, codes, queries, output_gradient, keys, values, r1, r2, before
        )
        before = (attn, dq)
        gathered += [own, rotated(t1, -1), rotated(t2, -2)]
    dk, dv = pl.pallas_call(
        functools.partial(finish, CHUNKS),
        name="finish",
        out_shape=[jax.ShapeDtypeStruct(keys.shape, jnp.bfloat16)] * 2,
    )(*gathered)
    return attn, dq, dk, dv


def solution(mesh):
    rows = P(("dp", "ctx"), None)
    return jax.shard_map(
        on_device,
        mesh=mesh,
        in_specs=(rows, rows, rows, rows, P("dp"), P("dp")),
        out_specs=(rows, rows, rows, rows),
        check_vma=False,
    )
```

time: 95 us -> 52.2 us (0.55)
  the two profiles are of different devices: /device:TPU:27 before, /device:TPU:0 now
where the time goes in v1:
time: 52.2 us; the launch traced here: 52 us
  waiting for transfers between devices  13.6 us (26%)
  starting transfers between devices  13.5 us (26%)
  Pallas kernels  11.3 us (22%)
  blocking collectives  8.6 us (16%)
  local copies, waits for them, and re-layouts  4.35 us (8%)
  between operations  0.69 us (1%)
    ppermute x8, waiting for transfers between devices, rotated(): lax.ppermute(array, AXES, [(i, (i + by) % count) for i in range(count)])  13.6 us
    ppermute x8, starting transfers between devices, rotated(): lax.ppermute(array, AXES, [(i, (i + by) % count) for i in range(count)])  13.5 us
    pallas_call x2, Pallas kernels, call_attend(): pl.pallas_call(functools.partial(attend, heads), grid=(1,), name=f'attend...  9.28 us
    psum x1, blocking collectives, on_device(): codes = lax.psum(jnp.where(owner == lax.axis_index('dp'), spread, 0), 'dp')  8.6 us
    unnamed x20, local copies, waits for them, and re-layouts  3.3 us
    pallas_call x1, Pallas kernels, on_device(): pl.pallas_call(functools.partial(finish, CHUNKS), name='finish', out_shap...  1.97 us
  transfers between devices with their start and end apart: 8, of which 3 were waited for; matrix products, arithmetic and copies ran while one was open for 0% of the time, Pallas kernels for 18%

profile of v1, /device:TPU:0, one launch (start us, length us, event | category | flops | bytes accessed | tf_op | source)
XLA Modules:
  0.0 52.0 jit_solution(14555457035937156851)
XLA Ops:
  0.6 1.0 %fusion = (bf16[128,256]{1,0:T(8,128)(2,1)S(1)}, bf16[128,256]{1,0:T(8,128)(2,1)S(1)}, bf16[128,256]{1,0:T(8,128)(2,1)S(1)}, bf16[128,256]{1,0:T(8,128)(2,1)S(1)}) fusion(bf16[128,512]{1,0:T(8,128)(2,1)} %k0_ref.3, bf16[128,512]{1,0:T(8,128)(2,1)} %v0_ref.3), kind=kLoop, calls=%fused_computation.8 | loop fusion | bytes 524288 | tf_op jit(solution)/shard_map/slice | solution.py:164
  1.6 4.1 %collective-permute-start.1 = (bf16[256,256]{1,0:T(8,128)(2,1)S(1)}, bf16[256,256]{1,0:T(8,128)(2,1)S(1)}, u32[]{:S(2)}, u32[]{:S(2)}) collective-permute-start(bf16[256,256]{1,0:T(8,128)(2,1)S(1)} %pad_maximum_fusion), channel_id=1, source_target_pairs={{0,2},{1,3},{2,4},{3,5},{4,6},{5,7},{6,8},{7,9},{8,10},{9,11},{10,... | collective-permute-start | bytes 393224 | tf_op jit(solution)/shard_map/ppermute | solution.py:23
  5.7 1.6 %collective-permute-start = (bf16[256,256]{1,0:T(8,128)(2,1)S(1)}, bf16[256,256]{1,0:T(8,128)(2,1)S(1)}, u32[]{:S(2)}, u32[]{:S(2)}) collective-permute-start(bf16[256,256]{1,0:T(8,128)(2,1)S(1)} %pad_maximum_fusion), channel_id=1, source_target_pairs={{0,1},{1,2},{2,3},{3,4},{4,5},{5,6},{6,7},{7,8},{8,9},{9,10},{10,1... | collective-permute-start | bytes 393224 | tf_op jit(solution)/shard_map/ppermute | solution.py:23
  7.3 0.1 collective-permute-start.3
  7.5 1.9 %collective-permute-start.2 = (bf16[256,256]{1,0:T(8,128)(2,1)S(1)}, bf16[256,256]{1,0:T(8,128)(2,1)S(1)}, u32[]{:S(2)}, u32[]{:S(2)}) collective-permute-start(bf16[256,256]{1,0:T(8,128)(2,1)S(1)} %pad_maximum_fusion.1), channel_id=1, source_target_pairs={{0,1},{1,2},{2,3},{3,4},{4,5},{5,6},{6,7},{7,8},{8,9},{9,10},{10,1... | collective-permute-start | bytes 393224 | tf_op jit(solution)/shard_map/ppermute | solution.py:23
  9.4 0.0 copy-start.8
  9.4 0.0 copy-start.9
  9.4 0.7 %copy-done.8 = s32[2]{0:T(128)S(1)} copy-done((s32[2]{0:T(128)S(1)}, s32[2]{0:T(128)}, u32[]{:S(2)}) %copy-start.8) | copy-done | bytes 32
  10.0 0.0 copy-done.9
  10.0 0.1 tile.10
  10.1 8.6 %psum.7.codes_ref = s32[16]{0:T(128)} all-reduce(s32[16]{0:T(128)S(1)} %compare_select_fusion), channel_id=1, replica_groups=mesh['dp'=8,'ctx'=4] {'dp'}, use_global_device_ids=true, to_apply=%region_0.1 | all-reduce | flops 16 | bytes 128 | tf_op jit(solution)/shard_map/psum | solution.py:161
  18.7 5.6 %collective-permute-done.3.r2_ref = bf16[256,256]{1,0:T(8,128)(2,1)S(1)} collective-permute-done((bf16[256,256]{1,0:T(8,128)(2,1)S(1)}, bf16[256,256]{1,0:T(8,128)(2,1)S(1)}, u32[]{:S(2)}, u32[]{:S(2)}) %collective-permute-start.3) | collective-permute-done | bytes 131104 | tf_op jit(solution)/shard_map/ppermute | solution.py:23
  24.3 0.0 copy-start.6
  24.3 0.0 collective-permute-done.2.r1_ref
  24.3 0.7 %copy-done.6 = bf16[256,256]{1,0:T(8,128)(2,1)} copy-done((bf16[256,256]{1,0:T(8,128)(2,1)}, bf16[256,256]{1,0:T(8,128)(2,1)S(1)}, u32[]{:S(2)}) %copy-start.6) | copy-done | bytes 131096
  25.0 0.0 copy-start.7
  25.0 0.7 %copy-done.7 = bf16[256,256]{1,0:T(8,128)(2,1)} copy-done((bf16[256,256]{1,0:T(8,128)(2,1)}, bf16[256,256]{1,0:T(8,128)(2,1)S(1)}, u32[]{:S(2)}) %copy-start.7) | copy-done | bytes 131096
  25.6 4.6 %attend0.1 = (bf16[128,2048]{1,0:T(8,128)(2,1)}, bf16[128,2048]{1,0:T(8,128)(2,1)}, f32[256,256]{1,0:T(8,128)}, bf16[256,256]{1,0:T(8,128)(2,1)}, bf16[256,256]{1,0:T(8,128)(2,1)}) custom-call(s32[16]{0:T(128)} %psum.7.codes_ref, bf16[128,2048]{1,0:T(8,128)(2,1)} %q_ref.3, bf16[128,2048]{1,0:T(8,128)(2,1)} %do_ref.3, bf16[128,512]{1,0:T(8,128)(2,1)} %k0_ref.3, ...), custom_call_target="tpu_custom_call" | custom-call | flops 603979776 | bytes 1048576 | tf_op jit(solution)/shard_map/attend0/pallas_call | solution.py:120
  30.3 1.2 %collective-permute-start.4 = (bf16[256,256]{1,0:T(8,128)(2,1)}, bf16[256,256]{1,0:T(8,128)(2,1)S(1)}, u32[]{:S(2)}, u32[]{:S(2)}) collective-permute-start(bf16[256,256]{1,0:T(8,128)(2,1)} %get-tuple-element.21), channel_id=1, source_target_pairs={{0,31},{1,0},{2,1},{3,2},{4,3},{5,4},{6,5},{7,6},{8,7},{9,8},{10,9... | collective-permute-start | bytes 393224 | tf_op jit(solution)/shard_map/ppermute | solution.py:23
  31.5 1.3 %collective-permute-start.5 = (bf16[256,256]{1,0:T(8,128)(2,1)}, bf16[256,256]{1,0:T(8,128)(2,1)S(1)}, u32[]{:S(2)}, u32[]{:S(2)}) collective-permute-start(bf16[256,256]{1,0:T(8,128)(2,1)} %get-tuple-element.22), channel_id=1, source_target_pairs={{0,30},{1,31},{2,0},{3,1},{4,2},{5,3},{6,4},{7,5},{8,6},{9,7},{10,... | collective-permute-start | bytes 393224 | tf_op jit(solution)/shard_map/ppermute | solution.py:23
  32.8 0.0 collective-permute-done.1.r2_ref
  32.8 0.0 copy-start
  32.8 0.0 collective-permute-done.r1_ref
  32.8 0.0 copy-start.1
  32.8 0.6 %copy-done = bf16[256,256]{1,0:T(8,128)(2,1)} copy-done((bf16[256,256]{1,0:T(8,128)(2,1)}, bf16[256,256]{1,0:T(8,128)(2,1)S(1)}, u32[]{:S(2)}) %copy-start) | copy-done | bytes 131096
  33.4 0.0 copy-done.1
  33.5 4.6 %attend1.1 = (bf16[128,2048]{1,0:T(8,128)(2,1)}, bf16[128,2048]{1,0:T(8,128)(2,1)}, f32[256,256]{1,0:T(8,128)}, bf16[256,256]{1,0:T(8,128)(2,1)}, bf16[256,256]{1,0:T(8,128)(2,1)}) custom-call(s32[16]{0:T(128)} %psum.7.codes_ref, bf16[128,2048]{1,0:T(8,128)(2,1)} %q_ref.3, bf16[128,2048]{1,0:T(8,128)(2,1)} %do_ref.3, ...), custom_call_target="tpu_custom_call", output_to_operand_aliasing={{0}: (7, {}), {1}: (8, {})} | custom-call | flops 603979776 | bytes 1048576 | tf_op jit(solution)/shard_map/attend1/pallas_call | solution.py:120
  38.1 1.9 %collective-permute-start.6 = (bf16[256,256]{1,0:T(8,128)(2,1)}, bf16[256,256]{1,0:T(8,128)(2,1)S(1)}, u32[]{:S(2)}, u32[]{:S(2)}) collective-permute-start(bf16[256,256]{1,0:T(8,128)(2,1)} %get-tuple-element.24), channel_id=1, source_target_pairs={{0,31},{1,0},{2,1},{3,2},{4,3},{5,4},{6,5},{7,6},{8,7},{9,8},{10,9... | collective-permute-start | bytes 393224 | tf_op jit(solution)/shard_map/ppermute | solution.py:23
  40.0 1.4 %collective-permute-start.7 = (bf16[256,256]{1,0:T(8,128)(2,1)}, bf16[256,256]{1,0:T(8,128)(2,1)S(1)}, u32[]{:S(2)}, u32[]{:S(2)}) collective-permute-start(bf16[256,256]{1,0:T(8,128)(2,1)} %get-tuple-element.25), channel_id=1, source_target_pairs={{0,30},{1,31},{2,0},{3,1},{4,2},{5,3},{6,4},{7,5},{8,6},{9,7},{10,... | collective-permute-start | bytes 393224 | tf_op jit(solution)/shard_map/ppermute | solution.py:23
  41.4 0.0 collective-permute-done.4.refs_1_
  41.4 0.0 copy-start.2
  41.4 0.0 collective-permute-done.5.refs_2_
  41.4 0.0 copy-start.3
  41.4 2.9 %collective-permute-done.6.refs_4_ = bf16[256,256]{1,0:T(8,128)(2,1)S(1)} collective-permute-done((bf16[256,256]{1,0:T(8,128)(2,1)}, bf16[256,256]{1,0:T(8,128)(2,1)S(1)}, u32[]{:S(2)}, u32[]{:S(2)}) %collective-permute-start.6) | collective-permute-done | bytes 131104 | tf_op jit(solution)/shard_map/ppermute | solution.py:23
  44.3 0.0 copy-start.4
  44.3 5.1 %collective-permute-done.7.refs_5_ = bf16[256,256]{1,0:T(8,128)(2,1)S(1)} collective-permute-done((bf16[256,256]{1,0:T(8,128)(2,1)}, bf16[256,256]{1,0:T(8,128)(2,1)S(1)}, u32[]{:S(2)}, u32[]{:S(2)}) %collective-permute-start.7) | collective-permute-done | bytes 131104 | tf_op jit(solution)/shard_map/ppermute | solution.py:23
  49.4 0.0 copy-start.5
  49.4 0.0 copy-done.2
  49.4 0.0 copy-done.3
  49.4 0.0 copy-done.4
  49.4 0.6 %copy-done.5 = bf16[256,256]{1,0:T(8,128)(2,1)} copy-done((bf16[256,256]{1,0:T(8,128)(2,1)}, bf16[256,256]{1,0:T(8,128)(2,1)S(1)}, u32[]{:S(2)}) %copy-start.5) | copy-done | bytes 131096
  50.0 2.0 %finish.1 = (bf16[128,512]{1,0:T(8,128)(2,1)}, bf16[128,512]{1,0:T(8,128)(2,1)}) custom-call(f32[256,256]{1,0:T(8,128)} %get-tuple-element.20.refs_0_, bf16[256,256]{1,0:T(8,128)(2,1)} %copy-done.2, bf16[256,256]{1,0:T(8,128)(2,1)} %copy-done.3, f32[256,256]{1,0:T(8,128)} %get-tuple-element.23.refs_3_, bf16[256,256]{1,0:T(8,128)(2,1)} %copy-done.4, ...), custom_call_target="tpu_custom_call" | custom-call | tf_op jit(solution)/shard_map/finish/pallas_call | solution.py:178
  (5 shorter events, 0.0 us)
Async XLA Ops:
  1.6 31.2 %collective-permute-start.1 = (bf16[256,256]{1,0:T(8,128)(2,1)S(1)}, bf16[256,256]{1,0:T(8,128)(2,1)S(1)}, u32[]{:S(2)}, u32[]{:S(2)}) collective-permute-start(bf16[256,256]{1,0:T(8,128)(2,1)S(1)} %pad_maximum_fusion), channel_id=1, source_target_pairs={{0,2},{1,3},{2,4},{3,5},{4,6},{5,7},{6,8},{7,9},{8,10},{9,11},{10,... | collective-permute-start | bytes 393224 | tf_op jit(solution)/shard_map/ppermute | solution.py:23
  5.7 27.1 %collective-permute-start = (bf16[256,256]{1,0:T(8,128)(2,1)S(1)}, bf16[256,256]{1,0:T(8,128)(2,1)S(1)}, u32[]{:S(2)}, u32[]{:S(2)}) collective-permute-start(bf16[256,256]{1,0:T(8,128)(2,1)S(1)} %pad_maximum_fusion), channel_id=1, source_target_pairs={{0,1},{1,2},{2,3},{3,4},{4,5},{5,6},{6,7},{7,8},{8,9},{9,10},{10,1... | collective-permute-start | bytes 393224 | tf_op jit(solution)/shard_map/ppermute | solution.py:23
  7.3 17.0 %collective-permute-start.3 = (bf16[256,256]{1,0:T(8,128)(2,1)S(1)}, bf16[256,256]{1,0:T(8,128)(2,1)S(1)}, u32[]{:S(2)}, u32[]{:S(2)}) collective-permute-start(bf16[256,256]{1,0:T(8,128)(2,1)S(1)} %pad_maximum_fusion.1), channel_id=1, source_target_pairs={{0,2},{1,3},{2,4},{3,5},{4,6},{5,7},{6,8},{7,9},{8,10},{9,11},{10,... | collective-permute-start | bytes 393224 | tf_op jit(solution)/shard_map/ppermute | solution.py:23
  7.5 16.9 %collective-permute-start.2 = (bf16[256,256]{1,0:T(8,128)(2,1)S(1)}, bf16[256,256]{1,0:T(8,128)(2,1)S(1)}, u32[]{:S(2)}, u32[]{:S(2)}) collective-permute-start(bf16[256,256]{1,0:T(8,128)(2,1)S(1)} %pad_maximum_fusion.1), channel_id=1, source_target_pairs={{0,1},{1,2},{2,3},{3,4},{4,5},{5,6},{6,7},{7,8},{8,9},{9,10},{10,1... | collective-permute-start | bytes 393224 | tf_op jit(solution)/shard_map/ppermute | solution.py:23
  9.4 0.7 %copy-start.8 = (s32[2]{0:T(128)S(1)}, s32[2]{0:T(128)}, u32[]{:S(2)}) copy-start(s32[2]{0:T(128)} %param.11) | copy-start | bytes 28
  9.4 0.7 %copy-start.9 = (s32[2]{0:T(128)S(1)}, s32[2]{0:T(128)}, u32[]{:S(2)}) copy-start(s32[2]{0:T(128)} %param.10) | copy-start | bytes 28
  24.3 0.7 %copy-start.6 = (bf16[256,256]{1,0:T(8,128)(2,1)}, bf16[256,256]{1,0:T(8,128)(2,1)S(1)}, u32[]{:S(2)}) copy-start(bf16[256,256]{1,0:T(8,128)(2,1)S(1)} %collective-permute-done.3.r2_ref) | copy-start | bytes 393220
  25.0 0.7 %copy-start.7 = (bf16[256,256]{1,0:T(8,128)(2,1)}, bf16[256,256]{1,0:T(8,128)(2,1)S(1)}, u32[]{:S(2)}) copy-start(bf16[256,256]{1,0:T(8,128)(2,1)S(1)} %collective-permute-done.2.r1_ref) | copy-start | bytes 393220
  30.3 11.1 %collective-permute-start.4 = (bf16[256,256]{1,0:T(8,128)(2,1)}, bf16[256,256]{1,0:T(8,128)(2,1)S(1)}, u32[]{:S(2)}, u32[]{:S(2)}) collective-permute-start(bf16[256,256]{1,0:T(8,128)(2,1)} %get-tuple-element.21), channel_id=1, source_target_pairs={{0,31},{1,0},{2,1},{3,2},{4,3},{5,4},{6,5},{7,6},{8,7},{9,8},{10,9... | collective-permute-start | bytes 393224 | tf_op jit(solution)/shard_map/ppermute | solution.py:23
  31.5 9.9 %collective-permute-start.5 = (bf16[256,256]{1,0:T(8,128)(2,1)}, bf16[256,256]{1,0:T(8,128)(2,1)S(1)}, u32[]{:S(2)}, u32[]{:S(2)}) collective-permute-start(bf16[256,256]{1,0:T(8,128)(2,1)} %get-tuple-element.22), channel_id=1, source_target_pairs={{0,30},{1,31},{2,0},{3,1},{4,2},{5,3},{6,4},{7,5},{8,6},{9,7},{10,... | collective-permute-start | bytes 393224 | tf_op jit(solution)/shard_map/ppermute | solution.py:23
  32.8 0.7 %copy-start = (bf16[256,256]{1,0:T(8,128)(2,1)}, bf16[256,256]{1,0:T(8,128)(2,1)S(1)}, u32[]{:S(2)}) copy-start(bf16[256,256]{1,0:T(8,128)(2,1)S(1)} %collective-permute-done.1.r2_ref) | copy-start | bytes 393220
  32.8 0.7 %copy-start.1 = (bf16[256,256]{1,0:T(8,128)(2,1)}, bf16[256,256]{1,0:T(8,128)(2,1)S(1)}, u32[]{:S(2)}) copy-start(bf16[256,256]{1,0:T(8,128)(2,1)S(1)} %collective-permute-done.r1_ref) | copy-start | bytes 393220
  38.1 6.1 %collective-permute-start.6 = (bf16[256,256]{1,0:T(8,128)(2,1)}, bf16[256,256]{1,0:T(8,128)(2,1)S(1)}, u32[]{:S(2)}, u32[]{:S(2)}) collective-permute-start(bf16[256,256]{1,0:T(8,128)(2,1)} %get-tuple-element.24), channel_id=1, source_target_pairs={{0,31},{1,0},{2,1},{3,2},{4,3},{5,4},{6,5},{7,6},{8,7},{9,8},{10,9... | collective-permute-start | bytes 393224 | tf_op jit(solution)/shard_map/ppermute | solution.py:23
  40.0 9.4 %collective-permute-start.7 = (bf16[256,256]{1,0:T(8,128)(2,1)}, bf16[256,256]{1,0:T(8,128)(2,1)S(1)}, u32[]{:S(2)}, u32[]{:S(2)}) collective-permute-start(bf16[256,256]{1,0:T(8,128)(2,1)} %get-tuple-element.25), channel_id=1, source_target_pairs={{0,30},{1,31},{2,0},{3,1},{4,2},{5,3},{6,4},{7,5},{8,6},{9,7},{10,... | collective-permute-start | bytes 393224 | tf_op jit(solution)/shard_map/ppermute | solution.py:23
  41.4 8.0 %copy-start.2 = (bf16[256,256]{1,0:T(8,128)(2,1)}, bf16[256,256]{1,0:T(8,128)(2,1)S(1)}, u32[]{:S(2)}) copy-start(bf16[256,256]{1,0:T(8,128)(2,1)S(1)} %collective-permute-done.4.refs_1_) | copy-start | bytes 393220
  41.4 8.0 %copy-start.3 = (bf16[256,256]{1,0:T(8,128)(2,1)}, bf16[256,256]{1,0:T(8,128)(2,1)S(1)}, u32[]{:S(2)}) copy-start(bf16[256,256]{1,0:T(8,128)(2,1)S(1)} %collective-permute-done.5.refs_2_) | copy-start | bytes 393220
  44.3 5.1 %copy-start.4 = (bf16[256,256]{1,0:T(8,128)(2,1)}, bf16[256,256]{1,0:T(8,128)(2,1)S(1)}, u32[]{:S(2)}) copy-start(bf16[256,256]{1,0:T(8,128)(2,1)S(1)} %collective-permute-done.6.refs_4_) | copy-start | bytes 393220
  49.4 0.6 %copy-start.5 = (bf16[256,256]{1,0:T(8,128)(2,1)}, bf16[256,256]{1,0:T(8,128)(2,1)S(1)}, u32[]{:S(2)}) copy-start(bf16[256,256]{1,0:T(8,128)(2,1)S(1)} %collective-permute-done.7.refs_5_) | copy-start | bytes 393220

commit v2 on v1

v2 whole, which is shorter than its diff:
```python
import functools
import jax
import jax.numpy as jnp
from jax import lax
from jax.experimental import pallas as pl
from jax.experimental.pallas import tpu as pltpu
from jax.sharding import PartitionSpec as P

QUERY_HEADS = 16
KEY_VALUE_HEADS = 4
HEAD_SIZE = 128
GROUP = QUERY_HEADS // KEY_VALUE_HEADS
AXES = ("dp", "ctx")
LOG2E = 1.4426950408889634
NEG = -1e30
CHUNKS = 2
LANE_HEADS = 2


def rotated(array, by):
    count = lax.axis_size(AXES)
    return lax.ppermute(array, AXES, [(i, (i + by) % count) for i in range(count)])


def doc_bounds(info_ref, block, rows):
    docs = info_ref.shape[0] // 2

    def step(i, carry):
        start, first, end = carry
        after = start + info_ref[i]
        mine = (start <= block) & (block < after)
        first = jnp.where(mine, start, first)
        end = jnp.where(mine, after * rows - info_ref[docs + i], end)
        return after, first, end

    zero = jnp.int32(0)
    _, first, end = lax.fori_loop(0, docs, step, (zero, zero, zero), unroll=min(docs, 16))
    return first, end


def dot(a, b, contract):
    return lax.dot_general(
        a, b, ((contract[:1], contract[1:]), ((), ())), preferred_element_type=jnp.float32
    )


def attend(chunk, heads, info_ref, q_ref, do_ref, k0_ref, v0_ref, r1_ref, r2_ref, *rest):
    attn_ref, dq_ref, own_ref, t1_ref, t2_ref = rest[-5:]
    rows = q_ref.shape[0]
    size = HEAD_SIZE
    block = lax.axis_index("dp") * lax.axis_size("ctx") + lax.axis_index("ctx")
    first, end = doc_bounds(info_ref, block, rows)
    scale = HEAD_SIZE ** (-0.5)
    bias1 = jnp.where(first <= block - 1, 0.0, NEG).astype(jnp.float32)
    bias2 = jnp.where(first <= block - 2, 0.0, NEG).astype(jnp.float32)
    width = LANE_HEADS * rows
    key_at = lax.broadcasted_iota(jnp.int32, (rows, width), 0)
    query_at = lax.broadcasted_iota(jnp.int32, (rows, width), 1) % rows
    causal = jnp.where(key_at <= query_at, 0.0, NEG).astype(jnp.float32)
    lane = lax.broadcasted_iota(jnp.int32, (1, width), 1) % rows
    valid = block * rows + lane < end
    parts = GROUP // LANE_HEADS
    units = [(head, part) for head in range(heads) for part in range(parts)]

    def of_head(head):
        cols = slice(head * size, (head + 1) * size)
        mine = slice((chunk * heads + head) * size, (chunk * heads + head + 1) * size)
        key = jnp.concatenate([r2_ref[:rows, cols], r1_ref[:rows, cols], k0_ref[:, mine]], axis=0)
        value = jnp.concatenate([r2_ref[rows:, cols], r1_ref[rows:, cols], v0_ref[:, mine]], axis=0)
        return key, value

    def names_of(unit):
        head, part = unit
        start = (chunk * heads + head) * GROUP + part * LANE_HEADS
        return range(start, start + LANE_HEADS)

    def stacked(ref, unit):
        return jnp.concatenate([ref[:, n * size : (n + 1) * size] for n in names_of(unit)], axis=0)

    def products(unit):
        key, value = of_head(unit[0])
        return dot(key, stacked(q_ref, unit), (1, 1)), dot(value, stacked(do_ref, unit), (1, 1))

    def weights(score, dprob):
        score = score * (scale * LOG2E)
        s2 = score[:rows] + bias2
        s1 = score[rows : 2 * rows] + bias1
        s0 = score[2 * rows :] + causal
        peak = jnp.max(jnp.maximum(jnp.maximum(s2, s1), s0), axis=0, keepdims=True)
        e2, e1, e0 = jnp.exp2(s2 - peak), jnp.exp2(s1 - peak), jnp.exp2(s0 - peak)
        total = jnp.sum(e2 + e1 + e0, axis=0, keepdims=True)
        inverse = jnp.where(valid, 1.0 / total, 0.0)
        weight = jnp.concatenate([e2, e1, e0], axis=0) * inverse
        delta = jnp.sum(weight * dprob, axis=0, keepdims=True)
        dscore = (weight * (dprob - delta)).astype(jnp.bfloat16)
        return weight.astype(jnp.bfloat16), dscore

    sums = {}

    def outputs(unit, weight, dscore):
        head, part = unit
        key, value = of_head(head)
        out = dot(value, weight, (0, 0))
        dq = dot(key, dscore, (0, 0)) * scale
        for i, n in enumerate(names_of(unit)):
            at = slice(n * size, (n + 1) * size)
            lanes = slice(i * rows, (i + 1) * rows)
            attn_ref[:, at] = out[:, lanes].T.astype(jnp.bfloat16)
            dq_ref[:, at] = dq[:, lanes].T.astype(jnp.bfloat16)
        dv = dot(weight, stacked(do_ref, unit), (1, 0))
        dk = dot(dscore, stacked(q_ref, unit), (1, 0)) * scale
        if part:
            dk, dv = sums[head][0] + dk, sums[head][1] + dv
        sums[head] = dk, dv
        if part < parts - 1:
            return
        cols = slice(head * size, (head + 1) * size)
        t2_ref[:rows, cols] = dk[:rows].astype(jnp.bfloat16)
        t2_ref[rows:, cols] = dv[:rows].astype(jnp.bfloat16)
        t1_ref[:rows, cols] = dk[rows : 2 * rows].astype(jnp.bfloat16)
        t1_ref[rows:, cols] = dv[rows : 2 * rows].astype(jnp.bfloat16)
        own_ref[:rows, cols] = dk[2 * rows :]
        own_ref[rows:, cols] = dv[2 * rows :]

    ready = products(units[0])
    for i, unit in enumerate(units):
        upcoming = products(units[i + 1]) if i + 1 < len(units) else None
        outputs(unit, *weights(*ready))
        ready = upcoming


def placed(array):
    return pltpu.with_memory_space_constraint(array, pltpu.VMEM)


def call_attend(chunk, info, q, do, keys, values, r1, r2, before):
    rows, q_width = q.shape
    heads = KEY_VALUE_HEADS // CHUNKS
    wide = heads * GROUP * HEAD_SIZE
    narrow = heads * HEAD_SIZE
    bf16 = jnp.bfloat16
    vmem = pl.BlockSpec(memory_space=pltpu.VMEM)
    return pl.pallas_call(
        functools.partial(attend, chunk, heads),
        in_specs=[pl.BlockSpec(memory_space=pltpu.SMEM)] + [vmem] * 6 + [vmem] * len(before),
        out_specs=[vmem] * 5,
        out_shape=[
            pltpu.VMEM((rows, q_width), bf16),
            pltpu.VMEM((rows, q_width), bf16),
            pltpu.VMEM((2 * rows, narrow), jnp.float32),
            pltpu.VMEM((2 * rows, narrow), bf16),
            pltpu.VMEM((2 * rows, narrow), bf16),
        ],
        input_output_aliases={7 + i: i for i in range(len(before))},
        compiler_params=pltpu.CompilerParams(vmem_limit_bytes=20 << 20),
        cost_estimate=pl.CostEstimate(
            flops=12 * rows * 3 * rows * wide, bytes_accessed=8 * rows * wide, transcendentals=0
        ),
    )(info, *map(placed, (q, do, keys, values, r1, r2, *before)))


def finish(chunks, *refs):
    dk_ref, dv_ref = refs[-2:]
    rows = dk_ref.shape[0]
    for c in range(chunks):
        own, r1, r2 = refs[3 * c : 3 * c + 3]
        width = own.shape[1]
        total = own[...] + r1[...].astype(jnp.float32) + r2[...].astype(jnp.float32)
        dk_ref[:, c * width : (c + 1) * width] = total[:rows].astype(jnp.bfloat16)
        dv_ref[:, c * width : (c + 1) * width] = total[rows:].astype(jnp.bfloat16)


def body(queries, keys, values, output_gradient, doc_blocks, doc_pad):
    width = KEY_VALUE_HEADS * HEAD_SIZE // CHUNKS
    per = doc_blocks.shape[0]
    parts = lax.axis_size("dp")
    mine = jnp.arange(parts, dtype=jnp.int32)[:, None] == lax.axis_index("dp")
    info = jnp.concatenate(
        [jnp.where(mine, part[None, :], 0).reshape(per * parts) for part in (doc_blocks, doc_pad)]
    )
    info = lax.psum(info, "dp")
    payloads = [
        jnp.concatenate(
            [keys[:, c * width : (c + 1) * width], values[:, c * width : (c + 1) * width]], axis=0
        )
        for c in range(CHUNKS)
    ]
    arrived = []
    for p in payloads:
        near = rotated(p, 1)
        far = rotated(p, 2)
        arrived.append((near, far))
    before = ()
    gathered = []
    for c in range(CHUNKS):
        r1, r2 = arrived[c]
        attn, dq, own, t1, t2 = call_attend(
            c, info, queries, output_gradient, keys, values, r1, r2, before
        )
        before = (attn, dq)
        gathered += [own, rotated(t1, -1), rotated(t2, -2)]
    dk, dv = pl.pallas_call(
        functools.partial(finish, CHUNKS),
        name="finish",
        compiler_params=pltpu.CompilerParams(vmem_limit_bytes=20 << 20),
        out_shape=[jax.ShapeDtypeStruct(keys.shape, jnp.bfloat16)] * 2,
    )(*map(placed, gathered))
    return attn, dq, dk, dv


def solution(mesh):
    rows = P(("dp", "ctx"), None)
    return jax.shard_map(
        body,
        mesh=mesh,
        in_specs=(rows, rows, rows, rows, P("dp"), P("dp")),
        out_specs=(rows, rows, rows, rows),
        check_vma=False,
    )
```

time: 52.2 us -> 48.1 us (0.921)
  Pallas kernels: 11.3 us -> 5.42 us
  waiting for transfers between devices: 13.6 us -> 14.9 us
  starting transfers between devices: 13.5 us -> 14.2 us
  blocking collectives: 8.6 us -> 8.06 us
    pallas_call x3, Pallas kernels: 11.3 us -> 5.42 us  [the longest x2 4.66 us: call_attend(): pl.pallas_call(functools.partial(attend, chunk, heads), in_specs=[pl.Bloc...]
    ppermute x8, waiting for transfers between devices: 13.6 us -> 14.9 us  [rotated(): lax.ppermute(array, AXES, [(i, (i + by) % count) for i in range(count)])]
    ppermute x8, starting transfers between devices: 13.5 us -> 14.2 us  [rotated(): lax.ppermute(array, AXES, [(i, (i + by) % count) for i in range(count)])]
    psum x1, blocking collectives: 8.6 us -> 8.06 us  [body(): info = lax.psum(info, 'dp')]
    unnamed x20 -> x14, local copies, waits for them, and re-layouts: 3.3 us -> 3.3 us
  transfers between devices with their start and end apart: 8 -> 8, of which waited for: 3 -> 3; matrix products, arithmetic and copies ran while one was open for 0% -> 4% of each run, Pallas kernels for 18% -> 10%
where the time goes in v2:
time: 48.1 us; the launch traced here: 47.9 us
  waiting for transfers between devices  14.9 us (31%)
  starting transfers between devices  14.2 us (30%)
  blocking collectives  8.06 us (17%)
  Pallas kernels  5.42 us (11%)
  local copies, waits for them, and re-layouts  4.47 us (9%)
  between operations  0.7 us (1%)
    ppermute x8, waiting for transfers between devices, rotated(): lax.ppermute(array, AXES, [(i, (i + by) % count) for i in range(count)])  14.9 us
    ppermute x8, starting transfers between devices, rotated(): lax.ppermute(array, AXES, [(i, (i + by) % count) for i in range(count)])  14.2 us
    psum x1, blocking collectives, body(): info = lax.psum(info, 'dp')  8.06 us
    pallas_call x2, Pallas kernels, call_attend(): pl.pallas_call(functools.partial(attend, chunk, heads), in_specs=[pl.Bloc...  4.66 us
    unnamed x14, local copies, waits for them, and re-layouts  3.3 us
    slice x1, local copies, waits for them, and re-layouts, body(): keys[:, c * width:(c + 1) * width]  1.01 us
  transfers between devices with their start and end apart: 8, of which 3 were waited for; matrix products, arithmetic and copies ran while one was open for 4% of the time, Pallas kernels for 10%

profile of v2, /device:TPU:0, one launch (start us, length us, event | category | flops | bytes accessed | tf_op | source)
XLA Modules:
  0.0 47.9 jit_solution(10869723446993340490)
XLA Ops:
  0.6 0.0 copy-start.2
  0.6 1.0 %fusion = (bf16[128,256]{1,0:T(8,128)(2,1)S(1)}, bf16[128,256]{1,0:T(8,128)(2,1)S(1)}, bf16[128,256]{1,0:T(8,128)(2,1)S(1)}, bf16[128,256]{1,0:T(8,128)(2,1)S(1)}) fusion(bf16[128,512]{1,0:T(8,128)(2,1)} %k0_ref.3, bf16[128,512]{1,0:T(8,128)(2,1)} %v0_ref.3), kind=kLoop, calls=%fused_computation.6 | loop fusion | bytes 524288 | tf_op jit(solution)/shard_map/slice | solution.py:184
  1.7 4.1 %collective-permute-start.1 = (bf16[256,256]{1,0:T(8,128)(2,1)S(1)}, bf16[256,256]{1,0:T(8,128)(2,1)S(1)}, u32[]{:S(2)}, u32[]{:S(2)}) collective-permute-start(bf16[256,256]{1,0:T(8,128)(2,1)S(1)} %pad_maximum_fusion), channel_id=1, source_target_pairs={{0,2},{1,3},{2,4},{3,5},{4,6},{5,7},{6,8},{7,9},{8,10},{9,11},{10,... | collective-permute-start | bytes 393224 | tf_op jit(solution)/shard_map/ppermute | solution.py:22
  5.8 1.6 %collective-permute-start = (bf16[256,256]{1,0:T(8,128)(2,1)S(1)}, bf16[256,256]{1,0:T(8,128)(2,1)S(1)}, u32[]{:S(2)}, u32[]{:S(2)}) collective-permute-start(bf16[256,256]{1,0:T(8,128)(2,1)S(1)} %pad_maximum_fusion), channel_id=1, source_target_pairs={{0,1},{1,2},{2,3},{3,4},{4,5},{5,6},{6,7},{7,8},{8,9},{9,10},{10,1... | collective-permute-start | bytes 393224 | tf_op jit(solution)/shard_map/ppermute | solution.py:22
  7.4 0.0 copy-start
  7.4 0.0 copy-start.1
  7.4 0.1 collective-permute-start.3
  7.5 1.9 %collective-permute-start.2 = (bf16[256,256]{1,0:T(8,128)(2,1)S(1)}, bf16[256,256]{1,0:T(8,128)(2,1)S(1)}, u32[]{:S(2)}, u32[]{:S(2)}) collective-permute-start(bf16[256,256]{1,0:T(8,128)(2,1)S(1)} %pad_maximum_fusion.1), channel_id=1, source_target_pairs={{0,1},{1,2},{2,3},{3,4},{4,5},{5,6},{6,7},{7,8},{8,9},{9,10},{10,1... | collective-permute-start | bytes 393224 | tf_op jit(solution)/shard_map/ppermute | solution.py:22
  9.4 0.0 copy-start.4
  9.4 0.0 copy-start.5
  9.4 0.6 %copy-done.4 = s32[2]{0:T(128)S(1)} copy-done((s32[2]{0:T(128)S(1)}, s32[2]{0:T(128)}, u32[]{:S(2)}) %copy-start.4) | copy-done | bytes 32
  10.1 0.0 copy-done.5
  10.1 0.1 broadcast_select_fusion.1
  10.2 0.1 select_n.16
  10.3 0.1 select_n.18
  10.3 0.1 pad_add_fusion
  10.4 8.1 %psum.7.info_ref = s32[32]{0:T(128)S(1)} all-reduce(s32[32]{0:T(128)S(1)} %pad_add_fusion), channel_id=1, replica_groups=mesh['dp'=8,'ctx'=4] {'dp'}, use_global_device_ids=true, to_apply=%region_0.1 | all-reduce | flops 32 | bytes 256 | tf_op jit(solution)/shard_map/psum | solution.py:181
  18.5 5.9 %collective-permute-done.3.r2_ref = bf16[256,256]{1,0:T(8,128)(2,1)S(1)} collective-permute-done((bf16[256,256]{1,0:T(8,128)(2,1)S(1)}, bf16[256,256]{1,0:T(8,128)(2,1)S(1)}, u32[]{:S(2)}, u32[]{:S(2)}) %collective-permute-start.3) | collective-permute-done | bytes 131104 | tf_op jit(solution)/shard_map/ppermute | solution.py:22
  24.4 0.0 collective-permute-done.2.r1_ref
  24.4 0.0 copy-done.2
  24.4 0.0 copy-done
  24.4 0.0 copy-done.1
  24.4 0.0 copy-start.3
  24.4 1.0 %copy-done.3 = bf16[128,2048]{1,0:T(8,128)(2,1)S(1)} copy-done((bf16[128,2048]{1,0:T(8,128)(2,1)S(1)}, bf16[128,2048]{1,0:T(8,128)(2,1)}, u32[]{:S(2)}) %copy-start.3) | copy-done | bytes 524312
  25.4 2.3 %shard_map.93 = (bf16[128,2048]{1,0:T(8,128)(2,1)S(1)}, bf16[128,2048]{1,0:T(8,128)(2,1)S(1)}, f32[256,256]{1,0:T(8,128)S(1)}, bf16[256,256]{1,0:T(8,128)(2,1)S(1)}, bf16[256,256]{1,0:T(8,128)(2,1)S(1)}) custom-call(s32[32]{0:T(128)S(1)} %psum.7.info_ref, bf16[128,2048]{1,0:T(8,128)(2,1)S(1)} %copy-done.2, bf16[128,2048]{1,0:T(8,128)(2,1)S(1)} %copy-done.3, ...), custom_call_target="tpu_custom_call" | custom-call | flops 603979776 | bytes 1048576 | tf_op jit(solution)/shard_map/pallas_call | solution.py:143
  27.8 1.3 %collective-permute-start.4 = (bf16[256,256]{1,0:T(8,128)(2,1)S(1)}, bf16[256,256]{1,0:T(8,128)(2,1)S(1)}, u32[]{:S(2)}, u32[]{:S(2)}) collective-permute-start(bf16[256,256]{1,0:T(8,128)(2,1)S(1)} %get-tuple-element.21), channel_id=1, source_target_pairs={{0,31},{1,0},{2,1},{3,2},{4,3},{5,4},{6,5},{7,6},{8,7},{9,8},{10,9... | collective-permute-start | bytes 393224 | tf_op jit(solution)/shard_map/ppermute | solution.py:22
  29.0 2.0 %collective-permute-start.5 = (bf16[256,256]{1,0:T(8,128)(2,1)S(1)}, bf16[256,256]{1,0:T(8,128)(2,1)S(1)}, u32[]{:S(2)}, u32[]{:S(2)}) collective-permute-start(bf16[256,256]{1,0:T(8,128)(2,1)S(1)} %get-tuple-element.22), channel_id=1, source_target_pairs={{0,30},{1,31},{2,0},{3,1},{4,2},{5,3},{6,4},{7,5},{8,6},{9,7},{10,... | collective-permute-start | bytes 393224 | tf_op jit(solution)/shard_map/ppermute | solution.py:22
  31.0 0.0 collective-permute-done.1.r2_ref
  31.0 0.0 collective-permute-done.r1_ref
  31.0 2.3 %shard_map.94 = (bf16[128,2048]{1,0:T(8,128)(2,1)S(1)}, bf16[128,2048]{1,0:T(8,128)(2,1)S(1)}, f32[256,256]{1,0:T(8,128)S(1)}, bf16[256,256]{1,0:T(8,128)(2,1)S(1)}, bf16[256,256]{1,0:T(8,128)(2,1)S(1)}) custom-call(s32[32]{0:T(128)S(1)} %psum.7.info_ref, bf16[128,2048]{1,0:T(8,128)(2,1)S(1)} %copy-done.2, ...), custom_call_target="tpu_custom_call", output_to_operand_aliasing={{0}: (7, {}), {1}: (8, {})} | custom-call | flops 603979776 | bytes 1048576 | tf_op jit(solution)/shard_map/pallas_call | solution.py:143
  33.4 1.3 %collective-permute-start.6 = (bf16[256,256]{1,0:T(8,128)(2,1)S(1)}, bf16[256,256]{1,0:T(8,128)(2,1)S(1)}, u32[]{:S(2)}, u32[]{:S(2)}) collective-permute-start(bf16[256,256]{1,0:T(8,128)(2,1)S(1)} %get-tuple-element.24), channel_id=1, source_target_pairs={{0,31},{1,0},{2,1},{3,2},{4,3},{5,4},{6,5},{7,6},{8,7},{9,8},{10,9... | collective-permute-start | bytes 393224 | tf_op jit(solution)/shard_map/ppermute | solution.py:22
  34.6 2.0 %collective-permute-start.7 = (bf16[256,256]{1,0:T(8,128)(2,1)S(1)}, bf16[256,256]{1,0:T(8,128)(2,1)S(1)}, u32[]{:S(2)}, u32[]{:S(2)}) collective-permute-start(bf16[256,256]{1,0:T(8,128)(2,1)S(1)} %get-tuple-element.25), channel_id=1, source_target_pairs={{0,30},{1,31},{2,0},{3,1},{4,2},{5,3},{6,4},{7,5},{8,6},{9,7},{10,... | collective-permute-start | bytes 393224 | tf_op jit(solution)/shard_map/ppermute | solution.py:22
  36.6 0.8 %copy.14 = bf16[128,2048]{1,0:T(8,128)(2,1)} copy(bf16[128,2048]{1,0:T(8,128)(2,1)S(1)} %get-tuple-element.36) | data formatting | bytes 1048576
  37.4 0.8 %copy.15 = bf16[128,2048]{1,0:T(8,128)(2,1)} copy(bf16[128,2048]{1,0:T(8,128)(2,1)S(1)} %get-tuple-element.37) | data formatting | bytes 1048576
  38.2 0.0 collective-permute-done.4.refs_1_
  38.2 1.6 %collective-permute-done.5.refs_2_ = bf16[256,256]{1,0:T(8,128)(2,1)S(1)} collective-permute-done((bf16[256,256]{1,0:T(8,128)(2,1)S(1)}, bf16[256,256]{1,0:T(8,128)(2,1)S(1)}, u32[]{:S(2)}, u32[]{:S(2)}) %collective-permute-start.5) | collective-permute-done | bytes 131104 | tf_op jit(solution)/shard_map/ppermute | solution.py:22
  39.9 0.0 collective-permute-done.6.refs_4_
  39.9 7.3 %collective-permute-done.7.refs_5_ = bf16[256,256]{1,0:T(8,128)(2,1)S(1)} collective-permute-done((bf16[256,256]{1,0:T(8,128)(2,1)S(1)}, bf16[256,256]{1,0:T(8,128)(2,1)S(1)}, u32[]{:S(2)}, u32[]{:S(2)}) %collective-permute-start.7) | collective-permute-done | bytes 131104 | tf_op jit(solution)/shard_map/ppermute | solution.py:22
  47.2 0.8 %finish.1 = (bf16[128,512]{1,0:T(8,128)(2,1)}, bf16[128,512]{1,0:T(8,128)(2,1)}) custom-call(f32[256,256]{1,0:T(8,128)S(1)} %get-tuple-element.20.refs_0_, bf16[256,256]{1,0:T(8,128)(2,1)S(1)} %collective-permute-done.4.refs_1_, bf16[256,256]{1,0:T(8,128)(2,1)S(1)} %collective-permute-done.5.refs_2_, f32[256,256]{1,0:T(8,128)S(1)} %get-tuple-element.23.refs_3_, ...), custom_call_target="tpu_custom_call" | custom-call | tf_op jit(solution)/shard_map/finish/pallas_call | solution.py:202
  (3 shorter events, 0.0 us)
Async XLA Ops:
  0.6 23.7 %copy-start.2 = (bf16[128,2048]{1,0:T(8,128)(2,1)S(1)}, bf16[128,2048]{1,0:T(8,128)(2,1)}, u32[]{:S(2)}) copy-start(bf16[128,2048]{1,0:T(8,128)(2,1)} %q_ref.3) | copy-start | bytes 1572868
  1.7 29.3 %collective-permute-start.1 = (bf16[256,256]{1,0:T(8,128)(2,1)S(1)}, bf16[256,256]{1,0:T(8,128)(2,1)S(1)}, u32[]{:S(2)}, u32[]{:S(2)}) collective-permute-start(bf16[256,256]{1,0:T(8,128)(2,1)S(1)} %pad_maximum_fusion), channel_id=1, source_target_pairs={{0,2},{1,3},{2,4},{3,5},{4,6},{5,7},{6,8},{7,9},{8,10},{9,11},{10,... | collective-permute-start | bytes 393224 | tf_op jit(solution)/shard_map/ppermute | solution.py:22
  5.8 25.2 %collective-permute-start = (bf16[256,256]{1,0:T(8,128)(2,1)S(1)}, bf16[256,256]{1,0:T(8,128)(2,1)S(1)}, u32[]{:S(2)}, u32[]{:S(2)}) collective-permute-start(bf16[256,256]{1,0:T(8,128)(2,1)S(1)} %pad_maximum_fusion), channel_id=1, source_target_pairs={{0,1},{1,2},{2,3},{3,4},{4,5},{5,6},{6,7},{7,8},{8,9},{9,10},{10,1... | collective-permute-start | bytes 393224 | tf_op jit(solution)/shard_map/ppermute | solution.py:22
  7.4 17.0 %copy-start = (bf16[128,512]{1,0:T(8,128)(2,1)S(1)}, bf16[128,512]{1,0:T(8,128)(2,1)}, u32[]{:S(2)}) copy-start(bf16[128,512]{1,0:T(8,128)(2,1)} %k0_ref.3) | copy-start | bytes 393220
  7.4 17.0 %copy-start.1 = (bf16[128,512]{1,0:T(8,128)(2,1)S(1)}, bf16[128,512]{1,0:T(8,128)(2,1)}, u32[]{:S(2)}) copy-start(bf16[128,512]{1,0:T(8,128)(2,1)} %v0_ref.3) | copy-start | bytes 393220
  7.4 17.0 %collective-permute-start.3 = (bf16[256,256]{1,0:T(8,128)(2,1)S(1)}, bf16[256,256]{1,0:T(8,128)(2,1)S(1)}, u32[]{:S(2)}, u32[]{:S(2)}) collective-permute-start(bf16[256,256]{1,0:T(8,128)(2,1)S(1)} %pad_maximum_fusion.1), channel_id=1, source_target_pairs={{0,2},{1,3},{2,4},{3,5},{4,6},{5,7},{6,8},{7,9},{8,10},{9,11},{10,... | collective-permute-start | bytes 393224 | tf_op jit(solution)/shard_map/ppermute | solution.py:22
  7.5 16.8 %collective-permute-start.2 = (bf16[256,256]{1,0:T(8,128)(2,1)S(1)}, bf16[256,256]{1,0:T(8,128)(2,1)S(1)}, u32[]{:S(2)}, u32[]{:S(2)}) collective-permute-start(bf16[256,256]{1,0:T(8,128)(2,1)S(1)} %pad_maximum_fusion.1), channel_id=1, source_target_pairs={{0,1},{1,2},{2,3},{3,4},{4,5},{5,6},{6,7},{7,8},{8,9},{9,10},{10,1... | collective-permute-start | bytes 393224 | tf_op jit(solution)/shard_map/ppermute | solution.py:22
  9.4 0.7 %copy-start.4 = (s32[2]{0:T(128)S(1)}, s32[2]{0:T(128)}, u32[]{:S(2)}) copy-start(s32[2]{0:T(128)} %param.10) | copy-start | bytes 28
  9.4 0.7 %copy-start.5 = (s32[2]{0:T(128)S(1)}, s32[2]{0:T(128)}, u32[]{:S(2)}) copy-start(s32[2]{0:T(128)} %param.11) | copy-start | bytes 28
  24.4 1.0 %copy-start.3 = (bf16[128,2048]{1,0:T(8,128)(2,1)S(1)}, bf16[128,2048]{1,0:T(8,128)(2,1)}, u32[]{:S(2)}) copy-start(bf16[128,2048]{1,0:T(8,128)(2,1)} %do_ref.3) | copy-start | bytes 1572868
  27.8 10.4 %collective-permute-start.4 = (bf16[256,256]{1,0:T(8,128)(2,1)S(1)}, bf16[256,256]{1,0:T(8,128)(2,1)S(1)}, u32[]{:S(2)}, u32[]{:S(2)}) collective-permute-start(bf16[256,256]{1,0:T(8,128)(2,1)S(1)} %get-tuple-element.21), channel_id=1, source_target_pairs={{0,31},{1,0},{2,1},{3,2},{4,3},{5,4},{6,5},{7,6},{8,7},{9,8},{10,9... | collective-permute-start | bytes 393224 | tf_op jit(solution)/shard_map/ppermute | solution.py:22
  29.0 10.8 %collective-permute-start.5 = (bf16[256,256]{1,0:T(8,128)(2,1)S(1)}, bf16[256,256]{1,0:T(8,128)(2,1)S(1)}, u32[]{:S(2)}, u32[]{:S(2)}) collective-permute-start(bf16[256,256]{1,0:T(8,128)(2,1)S(1)} %get-tuple-element.22), channel_id=1, source_target_pairs={{0,30},{1,31},{2,0},{3,1},{4,2},{5,3},{6,4},{7,5},{8,6},{9,7},{10,... | collective-permute-start | bytes 393224 | tf_op jit(solution)/shard_map/ppermute | solution.py:22
  33.4 6.5 %collective-permute-start.6 = (bf16[256,256]{1,0:T(8,128)(2,1)S(1)}, bf16[256,256]{1,0:T(8,128)(2,1)S(1)}, u32[]{:S(2)}, u32[]{:S(2)}) collective-permute-start(bf16[256,256]{1,0:T(8,128)(2,1)S(1)} %get-tuple-element.24), channel_id=1, source_target_pairs={{0,31},{1,0},{2,1},{3,2},{4,3},{5,4},{6,5},{7,6},{8,7},{9,8},{10,9... | collective-permute-start | bytes 393224 | tf_op jit(solution)/shard_map/ppermute | solution.py:22
  34.6 12.5 %collective-permute-start.7 = (bf16[256,256]{1,0:T(8,128)(2,1)S(1)}, bf16[256,256]{1,0:T(8,128)(2,1)S(1)}, u32[]{:S(2)}, u32[]{:S(2)}) collective-permute-start(bf16[256,256]{1,0:T(8,128)(2,1)S(1)} %get-tuple-element.25), channel_id=1, source_target_pairs={{0,30},{1,31},{2,0},{3,1},{4,2},{5,3},{6,4},{7,5},{8,6},{9,7},{10,... | collective-permute-start | bytes 393224 | tf_op jit(solution)/shard_map/ppermute | solution.py:22
